TPU v7x, 256 devices: a whole 4x4x8 slice. The times are simulated.
256 devices in a mesh: row: 32 (over y_lo, z, core), col: 8 (over y_hi, x).
Axes of the slice: x: 4, y: 4 (y_hi: 2, y_lo: 2; y = y_hi * 2 + y_lo), z: 8, core: 2. Of those that a mesh axis runs over, the one named last changes fastest.
Arguments:
- features: bfloat16 [262144, 256], P(('row', 'col')), may hold values from -6 to 6
- tile_values: bfloat16 [32, 8, 256, 128, 128], P('row', 'col'), may hold values from -0.09375 to 0.09375
- tile_rows: int32 [32, 8, 256], P('row', 'col'), may hold values from 0 to 63
- tile_cols: int32 [32, 8, 256], P('row', 'col'), may hold values from 0 to 255
- tile_count: int32 [32, 8], P('row', 'col'), may hold values from 64 to 256, as said below
- weight: bfloat16 [256, 256], replicated, may hold values from -0.375 to 0.375
Outputs:
- layer_out: bfloat16 [262144, 256], P(('row', 'col'))
Inputs may be any that keep to these rules, and one draw needn't show every extreme that they name: `tile_count`: live slots of one row block and column group; some block is full in every draw.
All inputs are finite; a program needn't handle non-finite values.
Results may differ from a plain program's by a relative error of at most 0.015.
Values may be sent and summed in bfloat16 or wider, within the bound.
A program may use at most 128 MiB of HBM per device.

v0:
```python
import math
import jax
import jax.numpy as jnp
from jax import lax
from jax.sharding import PartitionSpec as P


def local(features, tile_values, tile_rows, tile_cols, tile_count, weight):
    slab_rows, width = features.shape
    tiles = tile_values.shape[2]
    side = tile_values.shape[3]
    values = tile_values.reshape(tiles, side, side)
    rows_idx = tile_rows.reshape(tiles)
    cols_idx = tile_cols.reshape(tiles)
    count = tile_count.reshape(())
    group = lax.all_gather(features, "row", axis=0, tiled=True)
    col_count = group.shape[0] // side
    col_tiles = group.reshape(col_count, side, width)
    n_cols = lax.axis_size("col")
    row_tiles = n_cols * slab_rows // side
    block_len = math.gcd(tiles, 64)

    def accumulate(turn, carry):
        start = turn * block_len
        vals = lax.dynamic_slice_in_dim(values, start, block_len, 0)
        picks = lax.dynamic_slice_in_dim(cols_idx, start, block_len, 0)
        targets = lax.dynamic_slice_in_dim(rows_idx, start, block_len, 0)
        inputs = jnp.take(col_tiles, picks, axis=0)
        products = jnp.einsum("kij,kjf->kif", vals, inputs, preferred_element_type=jnp.float32)
        live = (start + jnp.arange(block_len, dtype=jnp.int32) < count).astype(jnp.float32)
        products = products * live[:, None, None]
        return carry.at[targets].add(products)

    carry = lax.fori_loop(
        0, tiles // block_len, accumulate, jnp.zeros((row_tiles, side, width), jnp.float32)
    )
    rounded = lax.optimization_barrier(carry.reshape(row_tiles * side, width).astype(jnp.bfloat16))
    partial_value = rounded.astype(jnp.float32)
    total = lax.psum(partial_value.astype(jnp.bfloat16), "col").astype(jnp.float32)
    summed = lax.dynamic_slice_in_dim(total, lax.axis_index("col") * slab_rows, slab_rows, 0)
    aggregated = summed.astype(jnp.bfloat16)
    return jnp.dot(aggregated, weight, preferred_element_type=jnp.float32).astype(jnp.bfloat16)


def solution(mesh):
    return jax.shard_map(
        local,
        mesh=mesh,
        in_specs=(
            P(("row", "col"), None),
            P("row", "col", None, None, None),
            P("row", "col", None),
            P("row", "col", None),
            P("row", "col"),
            P(),
        ),
        out_specs=P(("row", "col"), None),
        check_vma=False,
    )
```

profile of v0, /device:TPU:1, one launch (start us, length us, event | category | flops | bytes accessed | tf_op | source)
XLA Modules:
  0.0 392.6 jit_solution(11642625156492963269)
XLA Ops:
  6.5 0.7 all-gather.2.cloned.1.call-update
  7.3 105.8 %all-gather.2.cloned.1.call-done = bf16[32768,256]{1,0:T(8,128)(2,1)} async-done(((bf16[1024,256]{1,0:T(8,128)(2,1)}), bf16[32768,256]{1,0:T(8,128)(2,1)}) %all-gather.2.cloned.1.call-update) | async-done | bytes 16777232 | tf_op jit(solution)/shard_map/all_gather | solution.py:16
  113.1 4.2 %broadcast_in_dim.37 = f32[64,128,256]{2,1,0:T(8,128)} broadcast(f32[]{:T(128)} %constant.62.clone.1), dimensions={} | broadcast | bytes 8388612 | tf_op jit(solution)/shard_map/broadcast_in_dim | solution.py:35
  117.4 145.0 %while.13 = (s32[]{:T(128)}, f32[64,128,256]{2,1,0:T(8,128)}, s32[256]{0:T(256)S(1)}, bf16[256,128,128]{2,1,0:T(8,128)(2,1)}, s32[256]{0:T(256)S(1)}, /*index=5*...) while((s32[]{:T(128)}, f32[64,128,256]{2,1,0:T(8,128)}, ...), condition=%wide.region_2.3_spmd, body=%wide.region_0.2_spmd.sunk | while | flops 543164160 | bytes 48241208 | solution.py:34
  117.4 0.1 compare_select_fusion.4
  117.4 0.7 compare_and_fusion.2
  118.2 8.6 %gather_fusion = bf16[64,128,256]{2,1,0:T(8,128)(2,1)} fusion(bf16[256,128,256]{2,1,0:T(8,128)(2,1)} %get-tuple-element.223, s32[1024]{0:T(1024)S(1)} %pad_clamp_fusion.2), kind=kCustom, calls=%fused_computation.clone.1 | custom fusion | bytes 8388864 | tf_op jit(solution)/shard_map/while/body/eval_jaxpr/jit(_take)/gather | solution.py:28
  126.8 7.4 %broadcast_multiply_fusion.2 = f32[64,128,256]{2,1,0:T(8,128)} fusion(f32[64]{0:T(128)S(1)} %get-tuple-element.193, bf16[64,128,256]{2,1,0:T(8,128)(2,1)} %gather_fusion, pred[64]{0:T(512)(128)(4,1)S(1)} %get-tuple-element.195, bf16[256,128,128]{2,1,0:T(8,128)(2,1)} %get-tuple-element.221, s32[]{:T(128)S(6)} %select_n.49), kind=kOutput, calls=%fused_computation.2.clone.1 | convolution fusion | flops 541065216 | bytes 14680388 | tf_op jit(solution)/shard_map/while/body/eval_jaxpr/kij,kjf->kif/dot_general | solution.py:29
  134.2 19.4 %scatter_fusion = f32[64,128,256]{2,1,0:T(8,128)} fusion(f32[64,128,256]{2,1,0:T(8,128)} %get-tuple-element.208, s32[64]{0:T(128)S(1)} %compare_select_fusion.4, f32[64,128,256]{2,1,0:T(8,128)} %broadcast_multiply_fusion.2), kind=kCustom, calls=%fused_computation.1.clone.1 | custom fusion | flops 2097152 | bytes 25166080 | tf_op jit(solution)/shard_map/while/body/eval_jaxpr/scatter-add | solution.py:32
  153.6 0.7 compare_and_fusion.2
  154.3 8.6 %gather_fusion = bf16[64,128,256]{2,1,0:T(8,128)(2,1)} fusion(bf16[256,128,256]{2,1,0:T(8,128)(2,1)} %get-tuple-element.223, s32[1024]{0:T(1024)S(1)} %pad_clamp_fusion.2), kind=kCustom, calls=%fused_computation.clone.1 | custom fusion | bytes 8388864 | tf_op jit(solution)/shard_map/while/body/eval_jaxpr/jit(_take)/gather | solution.py:28
  163.0 7.4 %broadcast_multiply_fusion.2 = f32[64,128,256]{2,1,0:T(8,128)} fusion(f32[64]{0:T(128)S(1)} %get-tuple-element.193, bf16[64,128,256]{2,1,0:T(8,128)(2,1)} %gather_fusion, pred[64]{0:T(512)(128)(4,1)S(1)} %get-tuple-element.195, bf16[256,128,128]{2,1,0:T(8,128)(2,1)} %get-tuple-element.221, s32[]{:T(128)S(6)} %select_n.49), kind=kOutput, calls=%fused_computation.2.clone.1 | convolution fusion | flops 541065216 | bytes 14680388 | tf_op jit(solution)/shard_map/while/body/eval_jaxpr/kij,kjf->kif/dot_general | solution.py:29
  170.4 19.4 %scatter_fusion = f32[64,128,256]{2,1,0:T(8,128)} fusion(f32[64,128,256]{2,1,0:T(8,128)} %get-tuple-element.208, s32[64]{0:T(128)S(1)} %compare_select_fusion.4, f32[64,128,256]{2,1,0:T(8,128)} %broadcast_multiply_fusion.2), kind=kCustom, calls=%fused_computation.1.clone.1 | custom fusion | flops 2097152 | bytes 25166080 | tf_op jit(solution)/shard_map/while/body/eval_jaxpr/scatter-add | solution.py:32
  189.9 0.7 compare_and_fusion.2
  190.6 8.6 %gather_fusion = bf16[64,128,256]{2,1,0:T(8,128)(2,1)} fusion(bf16[256,128,256]{2,1,0:T(8,128)(2,1)} %get-tuple-element.223, s32[1024]{0:T(1024)S(1)} %pad_clamp_fusion.2), kind=kCustom, calls=%fused_computation.clone.1 | custom fusion | bytes 8388864 | tf_op jit(solution)/shard_map/while/body/eval_jaxpr/jit(_take)/gather | solution.py:28
  199.2 7.4 %broadcast_multiply_fusion.2 = f32[64,128,256]{2,1,0:T(8,128)} fusion(f32[64]{0:T(128)S(1)} %get-tuple-element.193, bf16[64,128,256]{2,1,0:T(8,128)(2,1)} %gather_fusion, pred[64]{0:T(512)(128)(4,1)S(1)} %get-tuple-element.195, bf16[256,128,128]{2,1,0:T(8,128)(2,1)} %get-tuple-element.221, s32[]{:T(128)S(6)} %select_n.49), kind=kOutput, calls=%fused_computation.2.clone.1 | convolution fusion | flops 541065216 | bytes 14680388 | tf_op jit(solution)/shard_map/while/body/eval_jaxpr/kij,kjf->kif/dot_general | solution.py:29
  206.6 19.4 %scatter_fusion = f32[64,128,256]{2,1,0:T(8,128)} fusion(f32[64,128,256]{2,1,0:T(8,128)} %get-tuple-element.208, s32[64]{0:T(128)S(1)} %compare_select_fusion.4, f32[64,128,256]{2,1,0:T(8,128)} %broadcast_multiply_fusion.2), kind=kCustom, calls=%fused_computation.1.clone.1 | custom fusion | flops 2097152 | bytes 25166080 | tf_op jit(solution)/shard_map/while/body/eval_jaxpr/scatter-add | solution.py:32
  226.1 0.7 compare_and_fusion.2
  226.9 8.6 %gather_fusion = bf16[64,128,256]{2,1,0:T(8,128)(2,1)} fusion(bf16[256,128,256]{2,1,0:T(8,128)(2,1)} %get-tuple-element.223, s32[1024]{0:T(1024)S(1)} %pad_clamp_fusion.2), kind=kCustom, calls=%fused_computation.clone.1 | custom fusion | bytes 8388864 | tf_op jit(solution)/shard_map/while/body/eval_jaxpr/jit(_take)/gather | solution.py:28
  235.5 7.4 %broadcast_multiply_fusion.2 = f32[64,128,256]{2,1,0:T(8,128)} fusion(f32[64]{0:T(128)S(1)} %get-tuple-element.193, bf16[64,128,256]{2,1,0:T(8,128)(2,1)} %gather_fusion, pred[64]{0:T(512)(128)(4,1)S(1)} %get-tuple-element.195, bf16[256,128,128]{2,1,0:T(8,128)(2,1)} %get-tuple-element.221, s32[]{:T(128)S(6)} %select_n.49), kind=kOutput, calls=%fused_computation.2.clone.1 | convolution fusion | flops 541065216 | bytes 14680388 | tf_op jit(solution)/shard_map/while/body/eval_jaxpr/kij,kjf->kif/dot_general | solution.py:29
  242.9 19.5 %scatter_fusion = f32[64,128,256]{2,1,0:T(8,128)} fusion(f32[64,128,256]{2,1,0:T(8,128)} %get-tuple-element.208, s32[64]{0:T(128)S(1)} %compare_select_fusion.4, f32[64,128,256]{2,1,0:T(8,128)} %broadcast_multiply_fusion.2), kind=kCustom, calls=%fused_computation.1.clone.1 | custom fusion | flops 2097152 | bytes 25166080 | tf_op jit(solution)/shard_map/while/body/eval_jaxpr/scatter-add | solution.py:32
  262.4 5.9 %convert_element_type.28 = bf16[64,128,256]{2,1,0:T(8,128)(2,1)} convert(f32[64,128,256]{2,1,0:T(8,128)} %get-tuple-element.129) | non-fusion elementwise | flops 2097152 | bytes 12582912 | tf_op jit(solution)/shard_map/convert_element_type | solution.py:37
  268.4 115.3 %all-reduce.2.cloned.1.call-done = bf16[8192,256]{1,0:T(8,128)(2,1)} async-done(((bf16[8192,256]{1,0:T(8,128)(2,1)}), bf16[8192,256]{1,0:T(8,128)(2,1)}) %all-reduce.2.cloned.1.call-update) | async-done | bytes 4194320 | tf_op jit(solution)/shard_map/psum | solution.py:39
  383.7 2.1 convolution_convert_fusion
  (16 shorter events, 0.3 us)
Async XLA Ops:
  6.5 377.1 %copy-start = (bf16[256,256]{1,0:T(8,128)(2,1)S(1)}, bf16[256,256]{1,0:T(8,128)(2,1)}, u32[]{:S(2)}) copy-start(bf16[256,256]{1,0:T(8,128)(2,1)} %param.13) | copy-start | bytes 393220
  6.5 110.8 %copy-start.2 = (s32[1,1,256]{2,1,0:T(1,128)S(1)}, s32[1,1,256]{2,1,0:T(1,128)}, u32[]{:S(2)}) copy-start(s32[1,1,256]{2,1,0:T(1,128)} %param.10) | copy-start | bytes 3076
  6.5 110.8 %copy-start.1 = (s32[1,1,256]{2,1,0:T(1,128)S(1)}, s32[1,1,256]{2,1,0:T(1,128)}, u32[]{:S(2)}) copy-start(s32[1,1,256]{2,1,0:T(1,128)} %param.11) | copy-start | bytes 3076
  6.5 106.6 %all-gather.2.cloned.1.call-start = ((), (), s32[]{:S(2)}) async-start(), calls=%async_computation | async-start | bytes 17301504 | tf_op jit(solution)/shard_map/all_gather | solution.py:16
  7.3 376.4 %all-reduce.2.cloned.1.call-start = ((), (), s32[]{:S(2)}) async-start(), calls=%async_computation.1 | async-start | bytes 8388608 | tf_op jit(solution)/shard_map/psum | solution.py:39
Sparse Core Ops, SparseCore 0:
  9.2 103.8 all-gather.1
  268.5 115.1 all-reduce.1
where the time goes:
time: 393 us
  waiting for transfers between devices  222 us (56%)
  other arithmetic  86.9 us (22%)
  local copies, waits for them, and re-layouts  38.8 us (10%)
  matrix products  31.6 us (8%)
  between operations  13.4 us (3%)
    psum x1, waiting for transfers between devices, local(): lax.psum(partial_value.astype(jnp.bfloat16), 'col').astype(jnp.float32)  115 us
    all_gather x1, waiting for transfers between devices, local(): group = lax.all_gather(features, 'row', axis=0, tiled=True)  106 us
    scatter-add x4, other arithmetic, accumulate(): return carry.at[targets].add(products)  77.8 us
    gather x4, local copies, waits for them, and re-layouts, accumulate(): inputs = jnp.take(col_tiles, picks, axis=0)  34.5 us
    dot_general x4, matrix products, accumulate(): jnp.einsum('kij,kjf->kif', vals, inputs, preferred_element_type=jnp.float32)  29.5 us
  transfers between devices with their start and end apart: 2, of which 2 were waited for; matrix products, arithmetic and copies ran while one was open for 0% of the time, Pallas kernels for 0%

commit v1 on v0

--- a/solution.py
+++ b/solution.py
@@ -13,7 +13,10 @@
     rows_idx = tile_rows.reshape(tiles)
     cols_idx = tile_cols.reshape(tiles)
     count = tile_count.reshape(())
-    group = lax.all_gather(features, "row", axis=0, tiled=True)
+    group = jnp.concatenate(
+        lax.all_to_all(jnp.stack([features for _ in range(lax.axis_size("row"))]), "row", 0, 0),
+        axis=0,
+    )
     col_count = group.shape[0] // side
     col_tiles = group.reshape(col_count, side, width)
     n_cols = lax.axis_size("col")

time: 393 us -> 676 us (1.72)
  waiting for transfers between devices: 222 us -> 486 us
  starting transfers between devices: 0.04 us -> 11.2 us
  local copies, waits for them, and re-layouts: 38.8 us -> 45.6 us
    all_to_all x0 -> x1, waiting for transfers between devices: none -> 361 us  [local(): lax.all_to_all(jnp.stack([features for _ in range(lax.axis_size('row'))])...]
    all_gather x1 -> x0, waiting for transfers between devices: 106 us -> none  [local(): group = lax.all_gather(features, 'row', axis=0, tiled=True)]
    all_to_all x0 -> x1, starting transfers between devices: none -> 11.2 us  [local(): lax.all_to_all(jnp.stack([features for _ in range(lax.axis_size('row'))])...]
    psum x1, waiting for transfers between devices: 115 us -> 125 us  [local(): lax.psum(partial_value.astype(jnp.bfloat16), 'col').astype(jnp.float32)]
    another operation x0 -> x1, local copies, waits for them, and re-layouts: none -> 6.81 us  [local(): jnp.stack([features for _ in range(lax.axis_size('row'))])]
where the time goes in v1:
time: 676 us; the launch traced here: 675 us
  waiting for transfers between devices  486 us (72%)
  other arithmetic  87.1 us (13%)
  local copies, waits for them, and re-layouts  45.6 us (7%)
  matrix products  31.6 us (5%)
  between operations  13.4 us (2%)
  starting transfers between devices  11.2 us (2%)
    all_to_all x1, waiting for transfers between devices, local(): lax.all_to_all(jnp.stack([features for _ in range(lax.axis_size('row'))])...  361 us
    psum x1, waiting for transfers between devices, local(): lax.psum(partial_value.astype(jnp.bfloat16), 'col').astype(jnp.float32)  125 us
    scatter-add x4, other arithmetic, accumulate(): return carry.at[targets].add(products)  77.9 us
    gather x4, local copies, waits for them, and re-layouts, accumulate(): inputs = jnp.take(col_tiles, picks, axis=0)  34.6 us
    dot_general x4, matrix products, accumulate(): jnp.einsum('kij,kjf->kif', vals, inputs, preferred_element_type=jnp.float32)  29.5 us
  transfers between devices with their start and end apart: 2, of which 2 were waited for; matrix products, arithmetic and copies ran while one was open for 0% of the time, Pallas kernels for 0%

profile of v1, /device:TPU:1, one launch (start us, length us, event | category | flops | bytes accessed | tf_op | source)
XLA Modules:
  0.0 675.2 jit_solution(9471773652205910320)
XLA Ops:
  6.5 6.8 %stack.2 = bf16[32,1024,256]{2,1,0:T(8,128)(2,1)} broadcast(bf16[1024,256]{1,0:T(8,128)(2,1)} %param.8), dimensions={1,2} | broadcast | bytes 17301504 | tf_op jit(solution)/shard_map/stack | solution.py:17
  13.3 11.2 %all-to-all-start = ((bf16[32,1024,256]{2,1,0:T(8,128)(2,1)}), bf16[32,1024,256]{2,1,0:T(8,128)(2,1)}, u32[]{:S(2)}, u32[]{:S(2)}) async-start(bf16[32,1024,256]{2,1,0:T(8,128)(2,1)} %stack.2), calls=%async_computation | async-start | bytes 33554432 | tf_op jit(solution)/shard_map/all_to_all | solution.py:17
  24.6 361.1 %all-to-all-done = bf16[32,1024,256]{2,1,0:T(8,128)(2,1)} async-done(((bf16[32,1024,256]{2,1,0:T(8,128)(2,1)}), bf16[32,1024,256]{2,1,0:T(8,128)(2,1)}, u32[]{:S(2)}, u32[]{:S(2)}) %all-to-all-start) | async-done | bytes 16777248 | tf_op jit(solution)/shard_map/all_to_all | solution.py:17
  385.7 4.2 broadcast_in_dim.37
  390.0 145.2 %while.13 = (s32[]{:T(128)}, f32[64,128,256]{2,1,0:T(8,128)}, s32[256]{0:T(256)S(1)}, bf16[256,128,128]{2,1,0:T(8,128)(2,1)}, s32[256]{0:T(256)S(1)}, /*index=5*...) while((s32[]{:T(128)}, f32[64,128,256]{2,1,0:T(8,128)}, ...), condition=%wide.region_2.3_spmd, body=%wide.region_0.2_spmd.sunk | while | flops 543164160 | bytes 48241200 | solution.py:37
  390.0 0.7 compare_and_fusion.2
  390.7 8.6 %gather_fusion = bf16[64,128,256]{2,1,0:T(8,128)(2,1)} fusion(bf16[256,128,256]{2,1,0:T(8,128)(2,1)} %get-tuple-element.223, s32[1024]{0:T(1024)S(1)} %pad_clamp_fusion.2), kind=kCustom, calls=%fused_computation.clone.1 | custom fusion | bytes 8388864 | tf_op jit(solution)/shard_map/while/body/eval_jaxpr/jit(_take)/gather | solution.py:31
  399.3 7.4 %broadcast_multiply_fusion.2 = f32[64,128,256]{2,1,0:T(8,128)} fusion(f32[64]{0:T(128)S(1)} %get-tuple-element.193, bf16[64,128,256]{2,1,0:T(8,128)(2,1)} %gather_fusion, pred[64]{0:T(512)(128)(4,1)S(1)} %get-tuple-element.195, bf16[256,128,128]{2,1,0:T(8,128)(2,1)} %get-tuple-element.221, s32[]{:T(128)S(6)} %select_n.49), kind=kOutput, calls=%fused_computation.2.clone.1 | convolution fusion | flops 541065216 | bytes 14680388 | tf_op jit(solution)/shard_map/while/body/eval_jaxpr/kij,kjf->kif/dot_general | solution.py:32
  406.8 19.5 %scatter_fusion = f32[64,128,256]{2,1,0:T(8,128)} fusion(f32[64,128,256]{2,1,0:T(8,128)} %get-tuple-element.208, s32[64]{0:T(128)S(1)} %compare_select_fusion.4, f32[64,128,256]{2,1,0:T(8,128)} %broadcast_multiply_fusion.2), kind=kCustom, calls=%fused_computation.1.clone.1 | custom fusion | flops 2097152 | bytes 25166080 | tf_op jit(solution)/shard_map/while/body/eval_jaxpr/scatter-add | solution.py:35
  426.3 0.7 compare_and_fusion.2
  427.0 8.6 %gather_fusion = bf16[64,128,256]{2,1,0:T(8,128)(2,1)} fusion(bf16[256,128,256]{2,1,0:T(8,128)(2,1)} %get-tuple-element.223, s32[1024]{0:T(1024)S(1)} %pad_clamp_fusion.2), kind=kCustom, calls=%fused_computation.clone.1 | custom fusion | bytes 8388864 | tf_op jit(solution)/shard_map/while/body/eval_jaxpr/jit(_take)/gather | solution.py:31
  435.6 7.4 %broadcast_multiply_fusion.2 = f32[64,128,256]{2,1,0:T(8,128)} fusion(f32[64]{0:T(128)S(1)} %get-tuple-element.193, bf16[64,128,256]{2,1,0:T(8,128)(2,1)} %gather_fusion, pred[64]{0:T(512)(128)(4,1)S(1)} %get-tuple-element.195, bf16[256,128,128]{2,1,0:T(8,128)(2,1)} %get-tuple-element.221, s32[]{:T(128)S(6)} %select_n.49), kind=kOutput, calls=%fused_computation.2.clone.1 | convolution fusion | flops 541065216 | bytes 14680388 | tf_op jit(solution)/shard_map/while/body/eval_jaxpr/kij,kjf->kif/dot_general | solution.py:32
  443.1 19.5 %scatter_fusion = f32[64,128,256]{2,1,0:T(8,128)} fusion(f32[64,128,256]{2,1,0:T(8,128)} %get-tuple-element.208, s32[64]{0:T(128)S(1)} %compare_select_fusion.4, f32[64,128,256]{2,1,0:T(8,128)} %broadcast_multiply_fusion.2), kind=kCustom, calls=%fused_computation.1.clone.1 | custom fusion | flops 2097152 | bytes 25166080 | tf_op jit(solution)/shard_map/while/body/eval_jaxpr/scatter-add | solution.py:35
  462.6 0.7 compare_and_fusion.2
  463.3 8.6 %gather_fusion = bf16[64,128,256]{2,1,0:T(8,128)(2,1)} fusion(bf16[256,128,256]{2,1,0:T(8,128)(2,1)} %get-tuple-element.223, s32[1024]{0:T(1024)S(1)} %pad_clamp_fusion.2), kind=kCustom, calls=%fused_computation.clone.1 | custom fusion | bytes 8388864 | tf_op jit(solution)/shard_map/while/body/eval_jaxpr/jit(_take)/gather | solution.py:31
  471.9 7.4 %broadcast_multiply_fusion.2 = f32[64,128,256]{2,1,0:T(8,128)} fusion(f32[64]{0:T(128)S(1)} %get-tuple-element.193, bf16[64,128,256]{2,1,0:T(8,128)(2,1)} %gather_fusion, pred[64]{0:T(512)(128)(4,1)S(1)} %get-tuple-element.195, bf16[256,128,128]{2,1,0:T(8,128)(2,1)} %get-tuple-element.221, s32[]{:T(128)S(6)} %select_n.49), kind=kOutput, calls=%fused_computation.2.clone.1 | convolution fusion | flops 541065216 | bytes 14680388 | tf_op jit(solution)/shard_map/while/body/eval_jaxpr/kij,kjf->kif/dot_general | solution.py:32
  479.4 19.4 %scatter_fusion = f32[64,128,256]{2,1,0:T(8,128)} fusion(f32[64,128,256]{2,1,0:T(8,128)} %get-tuple-element.208, s32[64]{0:T(128)S(1)} %compare_select_fusion.4, f32[64,128,256]{2,1,0:T(8,128)} %broadcast_multiply_fusion.2), kind=kCustom, calls=%fused_computation.1.clone.1 | custom fusion | flops 2097152 | bytes 25166080 | tf_op jit(solution)/shard_map/while/body/eval_jaxpr/scatter-add | solution.py:35
  498.8 0.7 compare_and_fusion.2
  499.6 8.6 %gather_fusion = bf16[64,128,256]{2,1,0:T(8,128)(2,1)} fusion(bf16[256,128,256]{2,1,0:T(8,128)(2,1)} %get-tuple-element.223, s32[1024]{0:T(1024)S(1)} %pad_clamp_fusion.2), kind=kCustom, calls=%fused_computation.clone.1 | custom fusion | bytes 8388864 | tf_op jit(solution)/shard_map/while/body/eval_jaxpr/jit(_take)/gather | solution.py:31
  508.2 7.4 %broadcast_multiply_fusion.2 = f32[64,128,256]{2,1,0:T(8,128)} fusion(f32[64]{0:T(128)S(1)} %get-tuple-element.193, bf16[64,128,256]{2,1,0:T(8,128)(2,1)} %gather_fusion, pred[64]{0:T(512)(128)(4,1)S(1)} %get-tuple-element.195, bf16[256,128,128]{2,1,0:T(8,128)(2,1)} %get-tuple-element.221, s32[]{:T(128)S(6)} %select_n.49), kind=kOutput, calls=%fused_computation.2.clone.1 | convolution fusion | flops 541065216 | bytes 14680388 | tf_op jit(solution)/shard_map/while/body/eval_jaxpr/kij,kjf->kif/dot_general | solution.py:32
  515.6 19.5 %scatter_fusion = f32[64,128,256]{2,1,0:T(8,128)} fusion(f32[64,128,256]{2,1,0:T(8,128)} %get-tuple-element.208, s32[64]{0:T(128)S(1)} %compare_select_fusion.4, f32[64,128,256]{2,1,0:T(8,128)} %broadcast_multiply_fusion.2), kind=kCustom, calls=%fused_computation.1.clone.1 | custom fusion | flops 2097152 | bytes 25166080 | tf_op jit(solution)/shard_map/while/body/eval_jaxpr/scatter-add | solution.py:35
  535.1 5.9 convert_element_type.28
  541.1 125.2 %all-reduce.2.cloned.1.call-done = bf16[8192,256]{1,0:T(8,128)(2,1)} async-done(((bf16[8192,256]{1,0:T(8,128)(2,1)}), bf16[8192,256]{1,0:T(8,128)(2,1)}) %all-reduce.2.cloned.1.call-update) | async-done | bytes 4194320 | tf_op jit(solution)/shard_map/psum | solution.py:42
  666.2 2.1 convolution_convert_fusion
  (16 shorter events, 0.4 us)
Async XLA Ops:
  6.5 659.7 %copy-start = (bf16[256,256]{1,0:T(8,128)(2,1)S(1)}, bf16[256,256]{1,0:T(8,128)(2,1)}, u32[]{:S(2)}) copy-start(bf16[256,256]{1,0:T(8,128)(2,1)} %param.13) | copy-start | bytes 393220
  13.3 372.4 %all-to-all-start = ((bf16[32,1024,256]{2,1,0:T(8,128)(2,1)}), bf16[32,1024,256]{2,1,0:T(8,128)(2,1)}, u32[]{:S(2)}, u32[]{:S(2)}) async-start(bf16[32,1024,256]{2,1,0:T(8,128)(2,1)} %stack.2), calls=%async_computation | async-start | bytes 33554432 | tf_op jit(solution)/shard_map/all_to_all | solution.py:17
  24.5 365.4 %copy-start.1 = (s32[1,1,256]{2,1,0:T(1,128)S(1)}, s32[1,1,256]{2,1,0:T(1,128)}, u32[]{:S(2)}) copy-start(s32[1,1,256]{2,1,0:T(1,128)} %param.11) | copy-start | bytes 3076
  24.5 365.4 %copy-start.2 = (s32[1,1,256]{2,1,0:T(1,128)S(1)}, s32[1,1,256]{2,1,0:T(1,128)}, u32[]{:S(2)}) copy-start(s32[1,1,256]{2,1,0:T(1,128)} %param.10) | copy-start | bytes 3076
  24.6 641.7 %all-reduce.2.cloned.1.call-start = ((), (), s32[]{:S(2)}) async-start(), calls=%async_computation.1 | async-start | bytes 8388608 | tf_op jit(solution)/shard_map/psum | solution.py:42
Sparse Core Ops, SparseCore 0:
  541.2 124.9 all-reduce.1
